TPU v7x, 256 devices: a whole 4x4x8 slice. The times are simulated.
256 devices in a mesh: seq: 64 (over z, x, core), fsdp: 4 (over y).
Axes of the slice: x: 4, y: 4, z: 8, core: 2. Of those that a mesh axis runs over, the one named last changes fastest.
Arguments:
- query_rows: bfloat16 [32768, 4096], P('seq', 'fsdp'), may hold values from -6 to 6
- key_rows: bfloat16 [32768, 4096], P('seq', 'fsdp'), may hold values from -0.5390625 to 0.5390625
- value_rows: bfloat16 [32768, 4096], P('seq', 'fsdp'), may hold values from -6 to 6
- norm_gain: float32 [4096], P('fsdp'), may hold values from 0.1 to 1.9
- out_weight: bfloat16 [4096, 4096], P(None, 'fsdp'), may hold values from -0.09375 to 0.09375
Outputs:
- mixed: bfloat16 [32768, 4096], P('seq', 'fsdp')
All inputs are finite; a program needn't handle non-finite values.
Results may differ from a plain program's by a relative error of at most 0.012.
Values may be sent and summed in bfloat16 or wider, within the bound.
No kernel may reach another device: no remote copies, remote signals or barrier semaphores. Data moves between devices by JAX's collectives and lax.ppermute only.
A program may use at most 192 MiB of HBM per device.

v0:
```python
import jax
import jax.numpy as jnp
from jax import lax
from jax.sharding import PartitionSpec as P

DH = 128
BLK = 512


def entering(value, axis, combine, identity):
    count, index = (lax.axis_size(axis), lax.axis_index(axis))
    everything = lax.all_gather(value, axis)
    start = jnp.broadcast_to(jnp.asarray(identity, value.dtype), value.shape)

    def step(k, before):
        reached = k < index
        new = combine(before, everything[k])
        return jnp.where(reached, new, before)

    return lax.fori_loop(0, count, step, start)


def add_states(earlier, later):
    return earlier + later


def earlier_states(local_total):
    return entering(local_total, "seq", add_states, jnp.zeros_like(local_total))


def shards(query_rows, key_rows, value_rows, norm_gain, out_weight):
    tokens = query_rows.shape[0]
    feature_width = query_rows.shape[1]
    heads_here = feature_width // DH
    n_blocks = tokens // BLK
    highest = lax.Precision.HIGHEST
    queries_b = query_rows.reshape(n_blocks, BLK, heads_here, DH)
    keys_b = key_rows.reshape(n_blocks, BLK, heads_here, DH)
    values_b = value_rows.reshape(n_blocks, BLK, heads_here, DH)
    block_state = jnp.einsum(
        "nkhd,nkhe->nhde", keys_b, values_b, preferred_element_type=jnp.float32
    )
    local_total = jnp.sum(block_state, axis=0)
    running_sum = jnp.cumsum(block_state, axis=0)
    local_before = jnp.concatenate([jnp.zeros_like(block_state), running_sum[:-1]], axis=0)
    position = lax.broadcasted_iota(jnp.int32, (BLK, BLK), 0)
    column = lax.broadcasted_iota(jnp.int32, (BLK, BLK), 1)
    causal_mask = column <= position
    queries_f = queries_b.astype(jnp.float32)
    prefix = earlier_states(local_total)
    carried = prefix[None] + local_before
    from_state = jnp.einsum("nqhd,nhde->nqhe", queries_f, carried, precision=highest)
    scores = jnp.einsum("nqhd,nkhd->nhqk", queries_b, keys_b, preferred_element_type=jnp.float32)
    masked_scores = jnp.where(causal_mask[None, None], scores, 0.0).astype(jnp.bfloat16)
    attention = (
        jnp.einsum("nhqk,nkhd->nqhd", masked_scores, values_b, preferred_element_type=jnp.float32)
        + from_state
    )
    mean_square = jnp.mean(attention * attention, axis=-1, keepdims=True)
    normed = attention * lax.rsqrt(mean_square + 1e-06) * norm_gain.reshape(heads_here, DH)
    normed = normed.astype(jnp.bfloat16).reshape(tokens, feature_width)
    summed = jnp.dot(
        lax.all_gather(normed, "fsdp", axis=1, tiled=True),
        out_weight,
        preferred_element_type=jnp.float32,
    )
    return summed.astype(jnp.bfloat16)


def solution(mesh):
    placed = (P("seq", "fsdp"), P("seq", "fsdp"), P("seq", "fsdp"), P("fsdp"), P(None, "fsdp"))
    return jax.shard_map(
        shards, mesh=mesh, in_specs=placed, out_specs=P("seq", "fsdp"), check_vma=False
    )
```

profile of v0, /device:TPU:1, one launch (start us, length us, event | category | flops | bytes accessed | tf_op | source)
XLA Modules:
  0.0 313.3 jit_solution(7516923831967842303)
XLA Ops:
  6.5 1.6 copy.17
  8.1 2.5 fusion.9
  10.8 146.7 %all-gather.6.cloned.1.call-done = f32[512,128,128]{2,1,0:T(8,128)} async-done(((f32[8,128,128]{2,1,0:T(8,128)}), f32[512,128,128]{2,1,0:T(8,128)}) %all-gather.6.cloned.1.call-update) | async-done | bytes 33554448 | tf_op jit(solution)/shard_map/all_gather | solution.py:12
  157.5 80.1 %while.14 = (s32[]{:T(128)}, f32[8,128,128]{2,1,0:T(8,128)S(1)}, s32[]{:T(128)}, f32[64,8,128,128]{3,2,1,0:T(8,128)}, s32[]{:T(128)}, /*index=5*/s32[]{:T(128)}) while((s32[]{:T(128)}, f32[8,128,128]{2,1,0:T(8,128)S(1)}, s32[]{:T(128)}, f32[64,8,128,128]{3,2,1,0:T(8,128)}, s32[]{:T(128)}, /*index=5*/s32[]{:T(128)}) %tuple.40), condition=%wide.region_1.0_spmd.clone, body=%wide.region_0.0_spmd.clone.sunk | while | flops 393220 | bytes 1572957 | solution.py:20
  158.7 1.2 add_select_fusion.2
  160.0 1.2 add_select_fusion.2
  161.2 1.2 add_select_fusion.2
  162.5 1.2 add_select_fusion.2
  163.7 1.2 add_select_fusion.2
  165.0 1.2 add_select_fusion.2
  166.2 1.2 add_select_fusion.2
  167.5 1.2 add_select_fusion.2
  168.7 1.2 add_select_fusion.2
  170.0 1.2 add_select_fusion.2
  171.2 1.2 add_select_fusion.2
  172.5 1.2 add_select_fusion.2
  173.8 1.2 add_select_fusion.2
  175.0 1.2 add_select_fusion.2
  176.3 1.2 add_select_fusion.2
  177.5 1.2 add_select_fusion.2
  178.8 1.2 add_select_fusion.2
  180.0 1.2 add_select_fusion.2
  181.3 1.2 add_select_fusion.2
  182.5 1.2 add_select_fusion.2
  183.8 1.2 add_select_fusion.2
  185.0 1.2 add_select_fusion.2
  186.3 1.2 add_select_fusion.2
  187.5 1.2 add_select_fusion.2
  188.8 1.2 add_select_fusion.2
  190.0 1.2 add_select_fusion.2
  191.3 1.2 add_select_fusion.2
  192.5 1.2 add_select_fusion.2
  193.8 1.2 add_select_fusion.2
  195.0 1.2 add_select_fusion.2
  196.3 1.2 add_select_fusion.2
  197.5 1.2 add_select_fusion.2
  198.8 1.2 add_select_fusion.2
  200.0 1.2 add_select_fusion.2
  201.3 1.2 add_select_fusion.2
  202.5 1.2 add_select_fusion.2
  203.8 1.2 add_select_fusion.2
  205.0 1.2 add_select_fusion.2
  206.3 1.2 add_select_fusion.2
  207.5 1.2 add_select_fusion.2
  208.8 1.2 add_select_fusion.2
  210.0 1.2 add_select_fusion.2
  211.3 1.2 add_select_fusion.2
  212.5 1.2 add_select_fusion.2
  213.8 1.2 add_select_fusion.2
  215.1 1.2 add_select_fusion.2
  216.3 1.2 add_select_fusion.2
  217.6 1.2 add_select_fusion.2
  218.8 1.2 add_select_fusion.2
  220.1 1.2 add_select_fusion.2
  221.3 1.2 add_select_fusion.2
  222.6 1.2 add_select_fusion.2
  223.8 1.2 add_select_fusion.2
  225.1 1.2 add_select_fusion.2
  226.3 1.2 add_select_fusion.2
  237.6 2.4 fusion.13
  240.0 5.9 %fusion.5 = (f32[512,8]{0,1:T(8,128)S(1)}, f32[8,128,512]{2,1,0:T(8,128)}) fusion(f32[8,128,512]{2,1,0:T(8,128)} %fusion.13, pred[512,512]{1,0:T(8,128)(4,1)S(1)} %iota_compare_fusion, bf16[512,8,128]{0,2,1:T(8,128)(2,1)S(1)} %bitcast.57, bf16[512,1024]{1,0:T(8,128)(2,1)} %param.9, bf16[512,1024]{1,0:T(8,128)(2,1)S(1)} %copy-done), kind=kOutput, calls=%fused_computation.8 | convolution fusion | flops 1079504896 | bytes 7618560 | tf_op jit(solution)/shard_map/nhqk,nkhd->nqhd/dot_general | solution.py:56
  245.9 2.8 fusion.7
  248.7 47.6 %all-gather.4.cloned.1.call-done = bf16[512,4096]{0,1:T(8,128)(2,1)} async-done(((bf16[512,1024]{0,1:T(8,128)(2,1)}), bf16[512,4096]{0,1:T(8,128)(2,1)}) %all-gather.4.cloned.1.call-update) | async-done | bytes 4194320 | tf_op jit(solution)/shard_map/all_gather | solution.py:63
  296.3 10.1 %convolution_convert_fusion = bf16[512,1024]{1,0:T(8,128)(2,1)} fusion(bf16[512,4096]{0,1:T(8,128)(2,1)} %all-gather.4.cloned.1.call-done, bf16[4096,1024]{1,0:T(8,128)(2,1)} %param.11), kind=kOutput, calls=%fused_computation.12 | convolution fusion | flops 4295491584 | bytes 13631488 | tf_op jit(solution)/shard_map/dot_general | solution.py:62
  (20 shorter events, 11.2 us)
Async XLA Ops:
  6.5 231.0 %copy-start = (bf16[512,1024]{1,0:T(8,128)(2,1)S(1)}, bf16[512,1024]{1,0:T(8,128)(2,1)}, u32[]{:S(2)}) copy-start(bf16[512,1024]{1,0:T(8,128)(2,1)} %param.7) | copy-start | bytes 3145732
  6.5 150.9 %all-gather.6.cloned.1.call-start = ((), (), s32[]{:S(2)}) async-start(), calls=%async_computation.1 | async-start | bytes 34078720 | tf_op jit(solution)/shard_map/all_gather | solution.py:12
  10.6 285.7 %all-gather.4.cloned.1.call-start = ((), (), s32[]{:S(2)}) async-start(), calls=%async_computation | async-start | bytes 5242880 | tf_op jit(solution)/shard_map/all_gather | solution.py:63
  240.0 5.9 %copy-start.1 = (f32[1024]{0:T(1024)S(1)}, f32[1024]{0:T(1024)}, u32[]{:S(2)}) copy-start(f32[1024]{0:T(1024)} %param.10) | copy-start | bytes 12292
Sparse Core Ops, SparseCore 0:
  10.7 146.6 all-gather.5
  248.8 47.4 all-gather.3
where the time goes:
time: 317 us; the launch traced here: 313 us
  waiting for transfers between devices  194 us (61%)
  other arithmetic  81.4 us (26%)
  matrix products  20.9 us (7%)
  between operations  13.5 us (4%)
    all_gather x1, waiting for transfers between devices, entering(): everything = lax.all_gather(value, axis)  147 us
    select_n x64, other arithmetic, step(): return jnp.where(reached, new, before)  78.5 us
    all_gather x1, waiting for transfers between devices, shards(): lax.all_gather(normed, 'fsdp', axis=1, tiled=True)  47.6 us
    dot_general x1, matrix products, shards(): jnp.dot(lax.all_gather(normed, 'fsdp', axis=1, tiled=True), out_weight, p...  10.1 us
  transfers between devices with their start and end apart: 2, of which 2 were waited for; matrix products, arithmetic and copies ran while one was open for 0% of the time, Pallas kernels for 0%

commit v1 on v0

--- a/solution.py
+++ b/solution.py
@@ -5,6 +5,12 @@
 
 DH = 128
 BLK = 512
+
+
+def gather_from_all(x, axis, dim):
+    size = lax.axis_size(axis)
+    repeats = [size if d == dim else 1 for d in range(x.ndim)]
+    return lax.all_to_all(jnp.tile(x, repeats), axis, split_axis=dim, concat_axis=dim, tiled=True)
 
 
 def entering(value, axis, combine, identity):
@@ -60,9 +66,7 @@
     normed = attention * lax.rsqrt(mean_square + 1e-06) * norm_gain.reshape(heads_here, DH)
     normed = normed.astype(jnp.bfloat16).reshape(tokens, feature_width)
     summed = jnp.dot(
-        lax.all_gather(normed, "fsdp", axis=1, tiled=True),
-        out_weight,
-        preferred_element_type=jnp.float32,
+        gather_from_all(normed, "fsdp", 1), out_weight, preferred_element_type=jnp.float32
     )
     return summed.astype(jnp.bfloat16)
 

time: 317 us -> 328 us (1.035)
  blocking collectives: 0 us -> 52.3 us
  waiting for transfers between devices: 194 us -> 147 us
  local copies, waits for them, and re-layouts: 1.59 us -> 8.9 us
    all_to_all x0 -> x1, blocking collectives: none -> 52.3 us  [gather_from_all(): lax.all_to_all(jnp.tile(x, repeats), axis, split_axis=dim, concat_axis=di...]
    all_gather x1 -> x0, waiting for transfers between devices: 47.6 us -> none  [shards(): lax.all_gather(normed, 'fsdp', axis=1, tiled=True)]
    all_to_all x0 -> x1, local copies, waits for them, and re-layouts: none -> 6.25 us  [gather_from_all(): lax.all_to_all(jnp.tile(x, repeats), axis, split_axis=dim, concat_axis=di...]
  transfers between devices with their start and end apart: 2 -> 1, of which waited for: 2 -> 1; matrix products, arithmetic and copies ran while one was open for 0% -> 0% of each run, Pallas kernels for 0% -> 0%
where the time goes in v1:
time: 328 us; the launch traced here: 324 us
  waiting for transfers between devices  147 us (45%)
  other arithmetic  80.5 us (25%)
  blocking collectives  52.3 us (16%)
  matrix products  20.9 us (6%)
  between operations  13.5 us (4%)
  local copies, waits for them, and re-layouts  8.9 us (3%)
    all_gather x1, waiting for transfers between devices, entering(): everything = lax.all_gather(value, axis)  147 us
    select_n x64, other arithmetic, step(): return jnp.where(reached, new, before)  78.5 us
    all_to_all x1, blocking collectives, gather_from_all(): lax.all_to_all(jnp.tile(x, repeats), axis, split_axis=dim, concat_axis=di...  52.3 us
    dot_general x1, matrix products, shards(): jnp.dot(gather_from_all(normed, 'fsdp', 1), out_weight, preferred_element...  10.2 us
  transfers between devices with their start and end apart: 1, of which 1 were waited for; matrix products, arithmetic and copies ran while one was open for 0% of the time, Pallas kernels for 0%

profile of v1, /device:TPU:1, one launch (start us, length us, event | category | flops | bytes accessed | tf_op | source)
XLA Modules:
  0.0 324.4 jit_solution(1492692982043100559)
XLA Ops:
  6.5 1.6 copy.28
  8.1 2.5 fusion.9
  10.7 146.8 %all-gather.3.cloned.1.call-done = f32[512,128,128]{2,1,0:T(8,128)} async-done(((f32[8,128,128]{2,1,0:T(8,128)}), f32[512,128,128]{2,1,0:T(8,128)}) %all-gather.3.cloned.1.call-update) | async-done | bytes 33554448 | tf_op jit(solution)/shard_map/all_gather | solution.py:18
  157.5 80.1 %while.14 = (s32[]{:T(128)}, f32[8,128,128]{2,1,0:T(8,128)S(1)}, s32[]{:T(128)}, f32[64,8,128,128]{3,2,1,0:T(8,128)}, s32[]{:T(128)}, /*index=5*/s32[]{:T(128)}) while((s32[]{:T(128)}, f32[8,128,128]{2,1,0:T(8,128)S(1)}, s32[]{:T(128)}, f32[64,8,128,128]{3,2,1,0:T(8,128)}, s32[]{:T(128)}, /*index=5*/s32[]{:T(128)}) %tuple.38), condition=%wide.region_1.0_spmd.clone, body=%wide.region_0.0_spmd.clone.sunk | while | flops 393220 | bytes 1572957 | solution.py:26
  158.7 1.2 add_select_fusion.2
  160.0 1.2 add_select_fusion.2
  161.2 1.2 add_select_fusion.2
  162.5 1.2 add_select_fusion.2
  163.7 1.2 add_select_fusion.2
  165.0 1.2 add_select_fusion.2
  166.2 1.2 add_select_fusion.2
  167.5 1.2 add_select_fusion.2
  168.7 1.2 add_select_fusion.2
  170.0 1.2 add_select_fusion.2
  171.2 1.2 add_select_fusion.2
  172.5 1.2 add_select_fusion.2
  173.8 1.2 add_select_fusion.2
  175.0 1.2 add_select_fusion.2
  176.3 1.2 add_select_fusion.2
  177.5 1.2 add_select_fusion.2
  178.8 1.2 add_select_fusion.2
  180.0 1.2 add_select_fusion.2
  181.3 1.2 add_select_fusion.2
  182.5 1.2 add_select_fusion.2
  183.8 1.2 add_select_fusion.2
  185.0 1.2 add_select_fusion.2
  186.3 1.2 add_select_fusion.2
  187.5 1.2 add_select_fusion.2
  188.8 1.2 add_select_fusion.2
  190.0 1.2 add_select_fusion.2
  191.3 1.2 add_select_fusion.2
  192.5 1.2 add_select_fusion.2
  193.8 1.2 add_select_fusion.2
  195.0 1.2 add_select_fusion.2
  196.3 1.2 add_select_fusion.2
  197.5 1.2 add_select_fusion.2
  198.8 1.2 add_select_fusion.2
  200.0 1.2 add_select_fusion.2
  201.3 1.2 add_select_fusion.2
  202.5 1.2 add_select_fusion.2
  203.8 1.2 add_select_fusion.2
  205.0 1.2 add_select_fusion.2
  206.3 1.2 add_select_fusion.2
  207.5 1.2 add_select_fusion.2
  208.8 1.2 add_select_fusion.2
  210.0 1.2 add_select_fusion.2
  211.3 1.2 add_select_fusion.2
  212.5 1.2 add_select_fusion.2
  213.8 1.2 add_select_fusion.2
  215.1 1.2 add_select_fusion.2
  216.3 1.2 add_select_fusion.2
  217.6 1.2 add_select_fusion.2
  218.8 1.2 add_select_fusion.2
  220.1 1.2 add_select_fusion.2
  221.3 1.2 add_select_fusion.2
  222.6 1.2 add_select_fusion.2
  223.8 1.2 add_select_fusion.2
  225.1 1.2 add_select_fusion.2
  237.6 2.4 fusion.11
  240.0 5.9 %fusion.5 = (f32[512,8]{0,1:T(8,128)S(1)}, f32[8,128,512]{2,1,0:T(8,128)}) fusion(f32[8,128,512]{2,1,0:T(8,128)} %fusion.11, pred[512,512]{1,0:T(8,128)(4,1)S(1)} %iota_compare_fusion, bf16[512,8,128]{0,2,1:T(8,128)(2,1)S(1)} %bitcast.59, bf16[512,1024]{1,0:T(8,128)(2,1)} %param.9, bf16[512,1024]{1,0:T(8,128)(2,1)S(1)} %copy-done), kind=kOutput, calls=%fused_computation.8 | convolution fusion | flops 1079504896 | bytes 7618560 | tf_op jit(solution)/shard_map/nhqk,nkhd->nqhd/dot_general | solution.py:62
  245.8 1.9 fusion.7
  248.8 52.3 %all_to_all.9 = bf16[512,4,1024]{2,0,1:T(8,128)(2,1)} all-to-all(bf16[512,4,1024]{2,0,1:T(8,128)(2,1)S(1)} %tile.9), channel_id=1, replica_groups=mesh['seq'=64,'fsdp'=4] {'fsdp'}, dimensions={1} | all-to-all | bytes 8388608 | tf_op jit(solution)/shard_map/all_to_all | solution.py:13
  301.1 6.3 %copy.26 = bf16[512,4,1024]{0,2,1:T(8,128)(2,1)} copy(bf16[512,4,1024]{2,0,1:T(8,128)(2,1)} %all_to_all.9) | data formatting | bytes 8388608 | tf_op jit(solution)/shard_map/all_to_all | solution.py:13
  307.3 10.2 %convolution_convert_fusion = bf16[512,1024]{1,0:T(8,128)(2,1)} fusion(bf16[512,4096]{0,1:T(8,128)(2,1)} %bitcast.57, bf16[4096,1024]{1,0:T(8,128)(2,1)} %param.11), kind=kOutput, calls=%fused_computation.12 | convolution fusion | flops 4295491584 | bytes 13631488 | tf_op jit(solution)/shard_map/dot_general | solution.py:68
  (23 shorter events, 13.4 us)
Async XLA Ops:
  6.5 231.0 %copy-start = (bf16[512,1024]{1,0:T(8,128)(2,1)S(1)}, bf16[512,1024]{1,0:T(8,128)(2,1)}, u32[]{:S(2)}) copy-start(bf16[512,1024]{1,0:T(8,128)(2,1)} %param.7) | copy-start | bytes 3145732
  6.5 150.9 %all-gather.3.cloned.1.call-start = ((), (), s32[]{:S(2)}) async-start(), calls=%async_computation.1 | async-start | bytes 34078720 | tf_op jit(solution)/shard_map/all_gather | solution.py:18
  239.9 5.9 %copy-start.2 = (f32[1024]{0:T(1024)S(1)}, f32[1024]{0:T(1024)}, u32[]{:S(2)}) copy-start(f32[1024]{0:T(1024)} %param.10) | copy-start | bytes 12292
  307.3 10.2 %copy-start.1 = (bf16[512,1024]{1,0:T(8,128)(2,1)S(1)}, bf16[512,1024]{1,0:T(8,128)(2,1)}, u32[]{:S(2)}) copy-start(bf16[512,1024]{1,0:T(8,128)(2,1)} %param.7) | copy-start | bytes 3145732
Sparse Core Ops, SparseCore 0:
  10.7 146.6 all-gather.2
